TPU v7x, 256 devices: a whole 4x4x8 slice. The times are simulated.
256 devices in a mesh: wide: 64 (over x, y, z_lo, core), narrow: 4 (over z_hi).
Axes of the slice: x: 4, y: 4, z: 8 (z_hi: 4, z_lo: 2; z = z_hi * 2 + z_lo), core: 2. Of those that a mesh axis runs over, the one named last changes fastest.
Arguments:
- volume: bfloat16 [64, 128, 32, 512], P(None, 'wide', 'narrow'), may hold values from -6 to 6
- out_grad: bfloat16 [64, 128, 32, 512], P(None, 'wide', 'narrow'), may hold values from -6 to 6
- plane_kernel: bfloat16 [9, 64, 64], replicated, may hold values from -0.25 to 0.25
- z_axis_kernel: bfloat16 [7, 64, 64], replicated, may hold values from -0.25 to 0.25
Outputs:
- volume_grad: bfloat16 [64, 128, 32, 512], P(None, 'wide', 'narrow')
- plane_kernel_grad: float32 [9, 64, 64], replicated
- z_axis_kernel_gradient: float32 [7, 64, 64], replicated
All inputs are finite; a program needn't handle non-finite values.
Results may differ from a plain program's by a relative error of at most 0.0061.
Values may be sent and summed in bfloat16 or wider, within the bound.
No kernel may reach another device: no remote copies, remote signals or barrier semaphores. Data moves between devices by JAX's collectives and lax.ppermute only.
A program may use at most 192 MiB of HBM per device.

v0:
```python
import functools
import math

import jax
import jax.numpy as jnp
from jax import lax
from jax.experimental import pallas as pl
from jax.experimental.pallas import tpu as pltpu
from jax.sharding import Mesh
from jax.sharding import PartitionSpec as P

LANES = 128
UNROLL = 16
SPREAD = ("wide_0", "wide_2", "wide_1")
WIDE = ("wide_0", "wide_1", "wide_2", "wide_3")
FLAT = ("wide_0", "wide_1")
TALL = ("wide_2", "wide_3", "narrow")
FACTORS = (4, 4, 2, 2)


def group_size(axes):
    return math.prod(lax.axis_size(a) for a in axes)


def halo_rows(first, last, axis):
    count = lax.axis_size(axis)
    forward = [(i, i + 1) for i in range(count - 1)]
    backward = [(i + 1, i) for i in range(count - 1)]
    return lax.ppermute(last, axis, forward), lax.ppermute(first, axis, backward)


def sigmoid(v):
    return 1.0 / (1.0 + jnp.exp(-v))


def shifted(block, step):
    width = block.shape[1]
    lane = lax.broadcasted_iota(jnp.int32, block.shape, 1)
    edge = 0 if step == 1 else width - 1
    return jnp.where(lane == edge, 0.0, pltpu.roll(block, step % width, 1))


def fill_rows(rows_ref, vol_ref, low_ref, high_ref):
    rows, slabs, width, _ = vol_ref.shape
    for z in range(slabs):
        rows_ref[z, 0:width, :] = low_ref[z]
        rows_ref[z, (rows + 1) * width :, :] = high_ref[z]

        def copy(x, carry, z=z):
            rows_ref[z, pl.ds(pl.multiple_of((x + 1) * width, width), width), :] = vol_ref[x, z]
            return carry

        lax.fori_loop(0, rows, copy, 0, unroll=True)


def plane_forward_kernel(
    vol_ref, low_ref, high_ref, w_ref, grad_ref, both_ref, slope_ref, rows_ref
):
    rows, slabs, width, cols = vol_ref.shape
    tiles = cols // LANES
    fill_rows(rows_ref, vol_ref, low_ref, high_ref)

    def step(n, carry):
        z, x = n // rows, n % rows
        window = rows_ref[z, pl.ds(pl.multiple_of(x * width, width), 3 * width), :]
        parts = jnp.dot(w_ref[...], window, preferred_element_type=jnp.float32)
        pre = (
            parts[width : 2 * width]
            + shifted(parts[:width], 1)
            + shifted(parts[2 * width :], -1)
        )
        gate = sigmoid(pre)
        slope_ref[z, x] = gate * (1.0 + pre * (1.0 - gate))
        act = (pre * gate).astype(jnp.bfloat16)
        for b in range(tiles):
            both_ref[x * tiles + b, z] = act[:, b * LANES : (b + 1) * LANES]
            both_ref[x * tiles + b, slabs + z] = grad_ref[x * tiles + b, z]
        return carry

    lax.fori_loop(0, slabs * rows, step, 0, unroll=UNROLL)


def peer_of(position, inner, outer):
    z, rest = position % inner, position // inner
    return (rest // outer) * (inner * outer) + z * outer + rest % outer


def depth_kernel(inner, outer, both_ref, wf_ref, wb_ref, out_ref, dw_ref, a_ref, d_ref, acc_ref):
    count, slabs, width, lanes = out_ref.shape
    rim = 3 * width
    cols = slabs * lanes
    zeros = jnp.zeros((rim, cols), jnp.bfloat16)
    for ref in (a_ref, d_ref):
        ref[0:rim, :] = zeros
        ref[rim + count * width :, :] = zeros
    acc_ref[...] = jnp.zeros_like(acc_ref)

    def fill(z, carry):
        for s in range(slabs):
            a_ref[
                pl.ds(pl.multiple_of(rim + z * width, width), width), s * lanes : (s + 1) * lanes
            ] = both_ref[peer_of(z, inner, outer), s]
        return carry

    lax.fori_loop(0, count, fill, 0, unroll=4)

    def forward(n, carry):
        base = pl.multiple_of(n * 2 * width, 2 * width)
        window = a_ref[pl.ds(base, 8 * width), :]
        depth = jnp.dot(wf_ref[...], window, preferred_element_type=jnp.float32)
        gate = sigmoid(depth)
        slope = gate * (1.0 + depth * (1.0 - gate))
        for a in range(2):
            for s in range(slabs):
                part = slope[a * width : (a + 1) * width, s * lanes : (s + 1) * lanes]
                grad = both_ref[peer_of(2 * n + a, inner, outer), slabs + s].astype(jnp.float32) * part
                at = pl.multiple_of(rim + base + a * width, width)
                d_ref[pl.ds(at, width), s * lanes : (s + 1) * lanes] = grad.astype(jnp.bfloat16)
        return carry

    lax.fori_loop(0, count // 2, forward, 0, unroll=UNROLL)

    def backward(n, carry):
        base = pl.multiple_of(n * 2 * width, 2 * width)
        back = jnp.dot(
            wb_ref[...], d_ref[pl.ds(base, 8 * width), :], preferred_element_type=jnp.float32
        ).astype(jnp.bfloat16)
        for a in range(2):
            for s in range(slabs):
                out_ref[peer_of(2 * n + a, inner, outer), s] = back[
                    a * width : (a + 1) * width, s * lanes : (s + 1) * lanes
                ]
        acc_ref[...] += lax.dot_general(
            d_ref[pl.ds(pl.multiple_of(rim + base, width), 2 * width), :],
            a_ref[pl.ds(base, 8 * width), :],
            (((1,), (1,)), ((), ())),
            preferred_element_type=jnp.float32,
        )
        return carry

    lax.fori_loop(0, count // 2, backward, 0, unroll=UNROLL)
    dw_ref[...] = acc_ref[0:width, :] + pltpu.roll(acc_ref[width:, :], 7 * width, 1)


def plane_grad_kernel(back_ref, slope_ref, rows_ref, dwz_ref, pre_ref, dw_ref, acc_ref):
    slabs, rows, width, cols = slope_ref.shape
    tiles = cols // LANES
    acc_ref[...] = jnp.zeros_like(acc_ref)

    def step(n, carry):
        z, x = n // rows, n % rows
        back = jnp.concatenate([back_ref[x * tiles + b, z] for b in range(tiles)], axis=1)
        grad = (back.astype(jnp.float32) * slope_ref[z, x]).astype(jnp.bfloat16)
        pre_ref[x, z] = grad
        wide = grad.astype(jnp.float32)
        stack = jnp.concatenate(
            [shifted(wide, -1).astype(jnp.bfloat16), grad, shifted(wide, 1).astype(jnp.bfloat16)],
            axis=0,
        )
        window = rows_ref[z, pl.ds(pl.multiple_of(x * width, width), 3 * width), :]
        acc_ref[...] += lax.dot_general(
            stack, window, (((1,), (1,)), ((), ())), preferred_element_type=jnp.float32
        )
        return carry

    lax.fori_loop(0, slabs * rows, step, 0, unroll=UNROLL)
    taps = [
        acc_ref[j * width : (j + 1) * width, i * width : (i + 1) * width]
        for i in range(3)
        for j in range(3)
    ] + [dwz_ref[:, k * width : (k + 1) * width] for k in range(7)]
    for p in range(8):
        dw_ref[p] = jnp.concatenate([taps[p], taps[p + 8]], axis=1)


def plane_backward_kernel(pre_ref, low_ref, high_ref, grad_ref, w_ref, out_ref, rows_ref):
    rows, slabs, width, cols = pre_ref.shape
    tiles = cols // LANES
    fill_rows(rows_ref, pre_ref, low_ref, high_ref)

    def step(n, carry):
        z, x = n // rows, n % rows
        window = rows_ref[z, pl.ds(pl.multiple_of(x * width, width), 3 * width), :]
        parts = jnp.dot(w_ref[...], window, preferred_element_type=jnp.float32)
        total = (
            parts[width : 2 * width]
            + shifted(parts[:width], -1)
            + shifted(parts[2 * width :], 1)
        )
        for b in range(tiles):
            lanes = slice(b * LANES, (b + 1) * LANES)
            grad = grad_ref[x * tiles + b, z].astype(jnp.float32)
            out_ref[x, z, :, lanes] = (total[:, lanes] + grad).astype(jnp.bfloat16)
        return carry

    lax.fori_loop(0, slabs * rows, step, 0, unroll=UNROLL)


def unpack_kernel(scale, total_ref, plane_ref, depth_ref):
    half = total_ref.shape[2] // 2
    for p in range(8):
        block = total_ref[p] * scale
        plane_ref[p] = block[:, :half]
        if p == 0:
            plane_ref[8] = block[:, half:]
        else:
            depth_ref[p - 1] = block[:, half:]


def call(kernel, outs, scratch=(), flops=0):
    vmem = pl.BlockSpec(memory_space=pltpu.VMEM)

    def run(*args):
        moved = sum(a.size * a.dtype.itemsize for a in (*args, *outs))
        return pl.pallas_call(
            kernel,
            out_shape=outs,
            in_specs=[vmem] * len(args),
            out_specs=[vmem] * len(outs),
            scratch_shapes=list(scratch),
            compiler_params=pltpu.CompilerParams(vmem_limit_bytes=16 << 20),
            cost_estimate=pl.CostEstimate(flops=flops, bytes_accessed=moved, transcendentals=0),
        )(*args)

    return run


def copies_kernel(pieces_ref, copies_ref):
    part = pieces_ref[0]
    for i in range(1, pieces_ref.shape[0]):
        part = part + pieces_ref[i]
    for i in range(copies_ref.shape[0]):
        copies_ref[i] = part


def spread_pieces(packed):
    pieces = packed.reshape(group_size(TALL), -1, LANES)
    return lax.all_to_all(pieces, TALL, 0, 0, tiled=True)


def copies_of(pieces, count):
    shape = jax.ShapeDtypeStruct((count, *pieces.shape[1:]), pieces.dtype)
    return call(copies_kernel, (shape,))(pieces)[0]


def on_device(volume, out_grad, plane_kernel, z_axis_kernel):
    width, slabs, rows, cols = volume.shape
    tiles = cols // LANES
    peers = group_size(SPREAD)
    shape = jax.ShapeDtypeStruct
    bf16, f32 = jnp.bfloat16, jnp.float32
    gradient_scale = 1.0 / math.sqrt(
        slabs * group_size(WIDE) * rows * lax.axis_size("narrow") * cols
    )
    blocks = (rows * tiles, slabs, width, LANES)

    slab = volume.transpose(2, 1, 0, 3)
    first, last = slab[0], slab[rows - 1]
    low, high = halo_rows(first, last, "narrow")


    grad_blocks = out_grad.reshape(width, slabs, rows, tiles, LANES)
    grad_blocks = grad_blocks.transpose(2, 3, 1, 0, 4).reshape(blocks)

    taps = plane_kernel.reshape(3, 3, width, width)
    plane_forward = taps.transpose(1, 2, 0, 3).reshape(3 * width, 3 * width)
    plane_backward = taps[::-1].transpose(1, 3, 0, 2).reshape(3 * width, 3 * width)
    none = jnp.zeros((1, width, width), bf16)

    def banded(tap_list):
        upper = jnp.concatenate([tap_list, none]).transpose(1, 0, 2).reshape(width, -1)
        lower = jnp.concatenate([none, tap_list]).transpose(1, 0, 2).reshape(width, -1)
        return jnp.concatenate([upper, lower])

    depth_forward = banded(z_axis_kernel)
    depth_backward = banded(z_axis_kernel[::-1].transpose(0, 2, 1))

    plane_flops = 2 * 9 * width * width * slabs * rows * cols
    depth_flops = plane_flops * 7 // 9
    low, high, plane_forward, plane_backward, depth_forward, depth_backward = (
        lax.optimization_barrier(
            (low, high, plane_forward, plane_backward, depth_forward, depth_backward)
        )
    )
    both, slope, rimmed = call(
        plane_forward_kernel,
        (
            shape((blocks[0], 2 * slabs, width, LANES), bf16),
            shape((slabs, rows, width, cols), f32),
            shape((slabs, (rows + 2) * width, cols), bf16),
        ),
        flops=plane_flops,
    )(slab, low, high, plane_forward, grad_blocks)

    both = lax.all_to_all(both, SPREAD, 0, 0, tiled=True)
    span = (peers + 6) * width
    back_pencil, depth_term = call(
        functools.partial(depth_kernel, lax.axis_size("wide_2"), lax.axis_size("wide_1")),
        (shape(blocks, bf16), shape((width, 8 * width), f32)),
        (
            pltpu.VMEM((span, slabs * LANES), bf16),
            pltpu.VMEM((span, slabs * LANES), bf16),
            pltpu.VMEM((2 * width, 8 * width), f32),
        ),
        flops=3 * depth_flops,
    )(both, depth_forward, depth_backward)
    back = lax.all_to_all(back_pencil, SPREAD, 0, 0, tiled=True)

    pre_grad, packed = call(
        plane_grad_kernel,
        (shape((rows, slabs, width, cols), bf16), shape((8, width, 2 * width), f32)),
        (pltpu.VMEM((3 * width, 3 * width), f32),),
        flops=plane_flops,
    )(back, slope, rimmed, depth_term)
    low, high = halo_rows(pre_grad[0], pre_grad[rows - 1], "narrow")
    pieces = spread_pieces(packed)
    pieces, plane_backward = lax.optimization_barrier((pieces, plane_backward))
    pieces = lax.all_to_all(copies_of(pieces, group_size(FLAT)), FLAT, 0, 0, tiled=True)
    (volume_grad,) = call(
        plane_backward_kernel,
        (shape((rows, slabs, width, cols), bf16),),
        (pltpu.VMEM((slabs, (rows + 2) * width, cols), bf16),),
        flops=plane_flops,
    )(pre_grad, low, high, grad_blocks, plane_backward)
    volume_grad = volume_grad.transpose(2, 1, 0, 3)
    pieces, volume_grad = lax.optimization_barrier((pieces, volume_grad))
    total = lax.all_to_all(copies_of(pieces, group_size(TALL)), TALL, 0, 0, tiled=True)
    plane_total, depth_total = call(
        functools.partial(unpack_kernel, gradient_scale),
        (shape((9, width, width), f32), shape((7, width, width), f32)),
    )(total.reshape(packed.shape))
    return volume_grad, plane_total, depth_total


def solution(mesh):
    names = WIDE + ("narrow",)
    finer = Mesh(mesh.devices.reshape(*FACTORS, mesh.shape["narrow"]), names)
    return jax.shard_map(
        on_device,
        mesh=finer,
        in_specs=(P(None, WIDE, "narrow", None), P(None, WIDE, "narrow", None), P(), P()),
        out_specs=(P(None, WIDE, "narrow", None), P(), P()),
        check_vma=False,
    )
```

profile of v0, /device:TPU:1, one launch (start us, length us, event | category | flops | bytes accessed | tf_op | source)
XLA Modules:
  0.0 137.2 jit_solution(4430334811639017082)
XLA Ops:
  0.7 1.8 %copy.29 = bf16[64,2,8,512]{3,0,1,2:T(8,128)(2,1)S(1)} copy(bf16[64,2,8,512]{3,2,1,0:T(8,128)(2,1)} %param.4) | data formatting | bytes 2097152 | tf_op args[0]
  2.5 0.7 slice_bitcast_fusion
  3.2 1.3 collective-permute-start.1
  4.5 6.3 %collective-permute-start = (bf16[2,64,512]{2,1,0:T(8,128)(2,1)}, bf16[2,64,512]{2,1,0:T(8,128)(2,1)S(1)}, u32[]{:S(2)}, u32[]{:S(2)}) collective-permute-start(bf16[2,64,512]{2,1,0:T(8,128)(2,1)} %get-tuple-element.50), channel_id=1, source_target_pairs={{0,1},{1,2},{2,3},{4,5},{5,6},{6,7},{8,9},{9,10},{10,11},{12,13},{... | collective-permute-start | bytes 393224 | tf_op jit(solution)/shard_map/ppermute | solution.py:29
  11.0 0.2 copy.18
  11.2 0.1 copy.30
  11.3 0.1 copy.25
  11.4 0.1 copy.26
  11.5 0.8 rev.6
  12.3 0.2 reshape.41.w_ref
  12.5 0.2 reshape.40.w_ref
  12.8 0.1 reshape.42
  12.9 0.1 copy.20
  13.0 0.1 reshape.43
  13.1 1.9 %copy.23 = bf16[64,2,8,4,128]{4,0,1,3,2:T(8,128)(2,1)S(1)} copy(bf16[64,2,8,4,128]{4,2,3,1,0:T(8,128)(2,1)} %bitcast.42) | data formatting | bytes 2097152 | tf_op jit(solution)/shard_map/reshape | solution.py:262
  15.1 1.6 %shard_map.67 = (bf16[32,4,64,128]{3,2,1,0:T(8,128)(2,1)S(1)}, f32[2,8,64,512]{3,2,1,0:T(8,128)S(1)}, bf16[2,640,512]{2,1,0:T(8,128)(2,1)S(1)}) custom-call(bf16[8,2,64,512]{3,2,1,0:T(8,128)(2,1)S(1)} %bitcast.38, bf16[2,64,512]{2,1,0:T(8,128)(2,1)S(1)} %collective-permute-done.low_ref, bf16[2,64,512]{2,1,0:T(8,128)(2,1)S(1)} %collective-permute-done.1.high_ref, ...), custom_call_target="tpu_custom_call" | custom-call | flops 603979776 | bytes 7938048 | tf_op jit(solution)/shard_map/pallas_call | solution.py:215
  16.7 36.8 %all_to_all.25.both_ref = bf16[32,4,64,128]{3,2,1,0:T(8,128)(2,1)S(1)} all-to-all(bf16[32,4,64,128]{3,2,1,0:T(8,128)(2,1)S(1)} %get-tuple-element.25), channel_id=1, replica_groups=mesh['wide_0'=4,'wide_1'=4,'wide_2'=2,'wide_3'=2,'narrow'=4] {'wide_0','..., dimensions={0} | all-to-all | bytes 4194304 | tf_op jit(solution)/shard_map/all_to_all | solution.py:295
  53.5 3.5 %shard_map.68 = (bf16[32,2,64,128]{3,2,1,0:T(8,128)(2,1)S(1)}, f32[64,512]{1,0:T(8,128)S(1)}) custom-call(bf16[32,4,64,128]{3,2,1,0:T(8,128)(2,1)S(1)} %all_to_all.25.both_ref, bf16[128,512]{1,0:T(8,128)(2,1)S(1)} %get-tuple-element.26.wf_ref, bf16[128,512]{1,0:T(8,128)(2,1)S(1)} %get-tuple-element.27.wb_ref), custom_call_target="tpu_custom_call" | custom-call | flops 1409286144 | bytes 3538944 | tf_op jit(solution)/shard_map/pallas_call | solution.py:215
  57.0 18.7 %all_to_all.26.back_ref = bf16[32,2,64,128]{3,2,1,0:T(8,128)(2,1)S(1)} all-to-all(bf16[32,2,64,128]{3,2,1,0:T(8,128)(2,1)S(1)} %get-tuple-element.28), channel_id=1, replica_groups=mesh['wide_0'=4,'wide_1'=4,'wide_2'=2,'wide_3'=2,'narrow'=4] {'wide_0','..., dimensions={0} | all-to-all | bytes 2097152 | tf_op jit(solution)/shard_map/all_to_all | solution.py:307
  75.7 1.3 shard_map.69
  77.0 21.6 %all_to_all.27.pieces_ref = f32[16,32,128]{2,1,0:T(8,128)S(1)} all-to-all(f32[16,32,128]{2,1,0:T(8,128)S(1)} %bitcast.41), channel_id=1, replica_groups=mesh['wide_0'=4,'wide_1'=4,'wide_2'=2,'wide_3'=2,'narrow'=4] {'wide_2','..., dimensions={0} | all-to-all | bytes 524288 | tf_op jit(solution)/shard_map/all_to_all | solution.py:238
  98.6 0.7 shard_map.70
  99.3 4.2 %all-to-all-start.3 = ((f32[16,32,128]{2,1,0:T(8,128)}), f32[16,32,128]{2,1,0:T(8,128)S(1)}, u32[]{:S(2)}, u32[]{:S(2)}) async-start(f32[16,32,128]{2,1,0:T(8,128)} %shard_map.70), calls=%async_computation.3 | async-start | bytes 524288 | tf_op jit(solution)/shard_map/all_to_all | solution.py:318
  103.6 1.3 collective-permute-start.3
  104.9 4.9 %collective-permute-start.2 = (bf16[2,64,512]{2,1,0:T(8,128)(2,1)S(1)}, bf16[2,64,512]{2,1,0:T(8,128)(2,1)S(1)}, u32[]{:S(2)}, u32[]{:S(2)}) collective-permute-start(bf16[2,64,512]{2,1,0:T(8,128)(2,1)S(1)} %get-tuple-element.48), channel_id=1, source_target_pairs={{0,1},{1,2},{2,3},{4,5},{5,6},{6,7},{8,9},{9,10},{10,11},{12,13},{... | collective-permute-start | bytes 393224 | tf_op jit(solution)/shard_map/ppermute | solution.py:29
  109.8 4.0 %collective-permute-done.3.high_ref = bf16[2,64,512]{2,1,0:T(8,128)(2,1)S(1)} collective-permute-done((bf16[2,64,512]{2,1,0:T(8,128)(2,1)S(1)}, bf16[2,64,512]{2,1,0:T(8,128)(2,1)S(1)}, u32[]{:S(2)}, u32[]{:S(2)}) %collective-permute-start.3) | collective-permute-done | bytes 131104 | tf_op jit(solution)/shard_map/ppermute | solution.py:29
  113.8 1.4 %shard_map.71 = bf16[8,2,64,512]{3,2,1,0:T(8,128)(2,1)S(1)} custom-call(bf16[8,2,64,512]{3,2,1,0:T(8,128)(2,1)S(1)} %get-tuple-element.35.pre_ref, bf16[2,64,512]{2,1,0:T(8,128)(2,1)S(1)} %collective-permute-done.2.low_ref, bf16[2,64,512]{2,1,0:T(8,128)(2,1)S(1)} %collective-permute-done.3.high_ref, bf16[32,2,64,128]{3,2,1,0:T(8,128)(2,1)S(1)} %bitcast.36, ...), custom_call_target="tpu_custom_call" | custom-call | flops 603979776 | bytes 3481600 | tf_op jit(solution)/shard_map/pallas_call | solution.py:215
  115.2 0.7 shard_map.72
  116.0 8.8 %all-to-all-start.4 = ((f32[16,32,128]{2,1,0:T(8,128)}), f32[16,32,128]{2,1,0:T(8,128)S(1)}, u32[]{:S(2)}, u32[]{:S(2)}) async-start(f32[16,32,128]{2,1,0:T(8,128)} %shard_map.72), calls=%async_computation.4 | async-start | bytes 524288 | tf_op jit(solution)/shard_map/all_to_all | solution.py:327
  124.7 1.5 %copy.24 = bf16[64,2,8,512]{3,2,1,0:T(8,128)(2,1)} copy(bf16[64,2,8,512]{3,0,1,2:T(8,128)(2,1)S(1)} %bitcast.39) | data formatting | bytes 2097152
  126.3 10.0 %all-to-all-done.4 = f32[16,32,128]{2,1,0:T(8,128)S(1)} async-done(((f32[16,32,128]{2,1,0:T(8,128)}), f32[16,32,128]{2,1,0:T(8,128)S(1)}, u32[]{:S(2)}, u32[]{:S(2)}) %all-to-all-start.4) | async-done | bytes 262176 | tf_op jit(solution)/shard_map/all_to_all | solution.py:327
  136.3 0.9 shard_map.73
  (14 shorter events, 0.2 us)
Async XLA Ops:
  0.6 10.2 %copy-start.1 = (bf16[7,64,64]{2,1,0:T(8,128)(2,1)S(1)}, bf16[7,64,64]{2,1,0:T(8,128)(2,1)}, u32[]{:S(2)}) copy-start(bf16[7,64,64]{2,1,0:T(8,128)(2,1)} %param.7) | copy-start | bytes 172036
  0.6 10.3 %copy-start = (bf16[9,64,64]{2,1,0:T(8,128)(2,1)S(1)}, bf16[9,64,64]{2,1,0:T(8,128)(2,1)}, u32[]{:S(2)}) copy-start(bf16[9,64,64]{2,1,0:T(8,128)(2,1)} %param.6) | copy-start | bytes 221188
  3.2 11.9 %collective-permute-start.1 = (bf16[2,64,512]{2,1,0:T(8,128)(2,1)}, bf16[2,64,512]{2,1,0:T(8,128)(2,1)S(1)}, u32[]{:S(2)}, u32[]{:S(2)}) collective-permute-start(bf16[2,64,512]{2,1,0:T(8,128)(2,1)} %get-tuple-element.49), channel_id=1, source_target_pairs={{1,0},{2,1},{3,2},{5,4},{6,5},{7,6},{9,8},{10,9},{11,10},{13,12},{... | collective-permute-start | bytes 393224 | tf_op jit(solution)/shard_map/ppermute | solution.py:29
  4.5 10.6 %collective-permute-start = (bf16[2,64,512]{2,1,0:T(8,128)(2,1)}, bf16[2,64,512]{2,1,0:T(8,128)(2,1)S(1)}, u32[]{:S(2)}, u32[]{:S(2)}) collective-permute-start(bf16[2,64,512]{2,1,0:T(8,128)(2,1)} %get-tuple-element.50), channel_id=1, source_target_pairs={{0,1},{1,2},{2,3},{4,5},{5,6},{6,7},{8,9},{9,10},{10,11},{12,13},{... | collective-permute-start | bytes 393224 | tf_op jit(solution)/shard_map/ppermute | solution.py:29
  99.3 15.9 %all-to-all-start.3 = ((f32[16,32,128]{2,1,0:T(8,128)}), f32[16,32,128]{2,1,0:T(8,128)S(1)}, u32[]{:S(2)}, u32[]{:S(2)}) async-start(f32[16,32,128]{2,1,0:T(8,128)} %shard_map.70), calls=%async_computation.3 | async-start | bytes 524288 | tf_op jit(solution)/shard_map/all_to_all | solution.py:318
  103.6 10.2 %collective-permute-start.3 = (bf16[2,64,512]{2,1,0:T(8,128)(2,1)S(1)}, bf16[2,64,512]{2,1,0:T(8,128)(2,1)S(1)}, u32[]{:S(2)}, u32[]{:S(2)}) collective-permute-start(bf16[2,64,512]{2,1,0:T(8,128)(2,1)S(1)} %get-tuple-element.47), channel_id=1, source_target_pairs={{1,0},{2,1},{3,2},{5,4},{6,5},{7,6},{9,8},{10,9},{11,10},{13,12},{... | collective-permute-start | bytes 393224 | tf_op jit(solution)/shard_map/ppermute | solution.py:29
  104.9 8.9 %collective-permute-start.2 = (bf16[2,64,512]{2,1,0:T(8,128)(2,1)S(1)}, bf16[2,64,512]{2,1,0:T(8,128)(2,1)S(1)}, u32[]{:S(2)}, u32[]{:S(2)}) collective-permute-start(bf16[2,64,512]{2,1,0:T(8,128)(2,1)S(1)} %get-tuple-element.48), channel_id=1, source_target_pairs={{0,1},{1,2},{2,3},{4,5},{5,6},{6,7},{8,9},{9,10},{10,11},{12,13},{... | collective-permute-start | bytes 393224 | tf_op jit(solution)/shard_map/ppermute | solution.py:29
  116.0 20.3 %all-to-all-start.4 = ((f32[16,32,128]{2,1,0:T(8,128)}), f32[16,32,128]{2,1,0:T(8,128)S(1)}, u32[]{:S(2)}, u32[]{:S(2)}) async-start(f32[16,32,128]{2,1,0:T(8,128)} %shard_map.72), calls=%async_computation.4 | async-start | bytes 524288 | tf_op jit(solution)/shard_map/all_to_all | solution.py:327
where the time goes:
time: 138 us; the launch traced here: 137 us
  blocking collectives  77 us (56%)
  starting transfers between devices  26.8 us (19%)
  waiting for transfers between devices  14 us (10%)
  Pallas kernels  10.2 us (7%)
  local copies, waits for them, and re-layouts  8.24 us (6%)
    all_to_all x1, blocking collectives, on_device(): both = lax.all_to_all(both, SPREAD, 0, 0, tiled=True)  36.8 us
    all_to_all x1, blocking collectives, spread_pieces(): return lax.all_to_all(pieces, TALL, 0, 0, tiled=True)  21.6 us
    all_to_all x1, blocking collectives, on_device(): back = lax.all_to_all(back_pencil, SPREAD, 0, 0, tiled=True)  18.7 us
    ppermute x2, starting transfers between devices, halo_rows(): lax.ppermute(last, axis, forward)  11.2 us
    pallas_call x7, Pallas kernels, run(): pl.pallas_call(kernel, out_shape=outs, in_specs=[vmem] * len(args), out_s...  10.2 us
    all_to_all x1, waiting for transfers between devices, on_device(): lax.all_to_all(copies_of(pieces, group_size(TALL)), TALL, 0, 0, tiled=True)  10 us
    all_to_all x1, starting transfers between devices, on_device(): lax.all_to_all(copies_of(pieces, group_size(TALL)), TALL, 0, 0, tiled=True)  8.78 us
    all_to_all x1, starting transfers between devices, on_device(): lax.all_to_all(copies_of(pieces, group_size(FLAT)), FLAT, 0, 0, tiled=True)  4.23 us
  transfers between devices with their start and end apart: 6, of which 2 were waited for; matrix products, arithmetic and copies ran while one was open for 4% of the time, Pallas kernels for 1%

commit v1 on v0

--- a/solution.py
+++ b/solution.py
@@ -13,8 +13,8 @@
 UNROLL = 16
 SPREAD = ("wide_0", "wide_2", "wide_1")
 WIDE = ("wide_0", "wide_1", "wide_2", "wide_3")
-FLAT = ("wide_0", "wide_1")
-TALL = ("wide_2", "wide_3", "narrow")
+FLAT = ("wide_0", "wide_1", "wide_3")
+TALL = ("wide_2", "narrow")
 FACTORS = (4, 4, 2, 2)
 
 
@@ -234,8 +234,8 @@
 
 
 def spread_pieces(packed):
-    pieces = packed.reshape(group_size(TALL), -1, LANES)
-    return lax.all_to_all(pieces, TALL, 0, 0, tiled=True)
+    pieces = packed.reshape(group_size(FLAT), -1, LANES)
+    return lax.all_to_all(pieces, FLAT, 0, 0, tiled=True)
 
 
 def copies_of(pieces, count):
@@ -314,8 +314,8 @@
     )(back, slope, rimmed, depth_term)
     low, high = halo_rows(pre_grad[0], pre_grad[rows - 1], "narrow")
     pieces = spread_pieces(packed)
+    pieces = lax.all_to_all(copies_of(pieces, group_size(TALL)), TALL, 0, 0, tiled=True)
     pieces, plane_backward = lax.optimization_barrier((pieces, plane_backward))
-    pieces = lax.all_to_all(copies_of(pieces, group_size(FLAT)), FLAT, 0, 0, tiled=True)
     (volume_grad,) = call(
         plane_backward_kernel,
         (shape((rows, slabs, width, cols), bf16),),
@@ -323,8 +323,7 @@
         flops=plane_flops,
     )(pre_grad, low, high, grad_blocks, plane_backward)
     volume_grad = volume_grad.transpose(2, 1, 0, 3)
-    pieces, volume_grad = lax.optimization_barrier((pieces, volume_grad))
-    total = lax.all_to_all(copies_of(pieces, group_size(TALL)), TALL, 0, 0, tiled=True)
+    total = lax.all_to_all(copies_of(pieces, group_size(FLAT)), FLAT, 0, 0, tiled=True)
     plane_total, depth_total = call(
         functools.partial(unpack_kernel, gradient_scale),
         (shape((9, width, width), f32), shape((7, width, width), f32)),

time: 138 us -> 127 us (0.920)
  the two profiles are of different devices: /device:TPU:1 before, /device:TPU:2 now
where the time goes in v1:
time: 127 us; the launch traced here: 126 us
  blocking collectives  84.5 us (67%)
  starting transfers between devices  18.9 us (15%)
  Pallas kernels  9.48 us (7%)
  local copies, waits for them, and re-layouts  7.54 us (6%)
  waiting for transfers between devices  4.51 us (4%)
    all_to_all x1, blocking collectives, on_device(): both = lax.all_to_all(both, SPREAD, 0, 0, tiled=True)  36.1 us
    all_to_all x1, blocking collectives, on_device(): back = lax.all_to_all(back_pencil, SPREAD, 0, 0, tiled=True)  20.1 us
    all_to_all x1, blocking collectives, on_device(): lax.all_to_all(copies_of(pieces, group_size(TALL)), TALL, 0, 0, tiled=True)  14.9 us
    all_to_all x1, blocking collectives, spread_pieces(): return lax.all_to_all(pieces, FLAT, 0, 0, tiled=True)  13.4 us
    ppermute x2, starting transfers between devices, halo_rows(): lax.ppermute(last, axis, forward)  11.3 us
    pallas_call x7, Pallas kernels, run(): pl.pallas_call(kernel, out_shape=outs, in_specs=[vmem] * len(args), out_s...  9.48 us
    all_to_all x1, starting transfers between devices, on_device(): lax.all_to_all(copies_of(pieces, group_size(FLAT)), FLAT, 0, 0, tiled=True)  5.02 us
    ppermute x2, waiting for transfers between devices, halo_rows(): lax.ppermute(first, axis, backward)  4.5 us
  transfers between devices with their start and end apart: 5, of which 2 were waited for; matrix products, arithmetic and copies ran while one was open for 5% of the time, Pallas kernels for 1%

profile of v1, /device:TPU:2, one launch (start us, length us, event | category | flops | bytes accessed | tf_op | source)
XLA Modules:
  0.0 125.8 jit_solution(1653861124037424714)
XLA Ops:
  0.7 1.8 %copy.29 = bf16[64,2,8,512]{3,0,1,2:T(8,128)(2,1)S(1)} copy(bf16[64,2,8,512]{3,2,1,0:T(8,128)(2,1)} %param.4) | data formatting | bytes 2097152 | tf_op args[0]
  2.5 1.3 %collective-permute-start.1 = (bf16[2,64,512]{2,1,0:T(8,128)(2,1)S(1)}, bf16[2,64,512]{2,1,0:T(8,128)(2,1)S(1)}, u32[]{:S(2)}, u32[]{:S(2)}) collective-permute-start(bf16[2,64,512]{2,1,0:T(8,128)(2,1)S(1)} %get-tuple-element.45), channel_id=1, source_target_pairs={{1,0},{2,1},{3,2},{5,4},{6,5},{7,6},{9,8},{10,9},{11,10},{13,12},{... | collective-permute-start | bytes 393224 | tf_op jit(solution)/shard_map/ppermute | solution.py:29
  3.8 5.8 %collective-permute-start = (bf16[2,64,512]{2,1,0:T(8,128)(2,1)S(1)}, bf16[2,64,512]{2,1,0:T(8,128)(2,1)S(1)}, u32[]{:S(2)}, u32[]{:S(2)}) collective-permute-start(bf16[2,64,512]{2,1,0:T(8,128)(2,1)S(1)} %get-tuple-element.46), channel_id=1, source_target_pairs={{0,1},{1,2},{2,3},{4,5},{5,6},{6,7},{8,9},{9,10},{10,11},{12,13},{... | collective-permute-start | bytes 393224 | tf_op jit(solution)/shard_map/ppermute | solution.py:29
  9.8 0.2 copy.18
  9.9 0.1 copy.30
  10.1 0.1 copy.25
  10.2 0.1 copy.26
  10.3 0.8 rev.6
  11.1 0.2 reshape.41.w_ref
  11.3 0.2 reshape.40.w_ref
  11.4 0.1 copy.19
  11.5 0.1 reshape.42
  11.7 0.1 copy.20
  11.8 0.1 reshape.43
  11.9 1.9 %copy.23 = bf16[64,2,8,4,128]{4,0,1,3,2:T(8,128)(2,1)S(1)} copy(bf16[64,2,8,4,128]{4,2,3,1,0:T(8,128)(2,1)} %bitcast.42) | data formatting | bytes 2097152 | tf_op jit(solution)/shard_map/reshape | solution.py:262
  13.9 0.1 collective-permute-done.1.high_ref
  14.0 0.0 collective-permute-done.low_ref
  14.0 1.6 %shard_map.67 = (bf16[32,4,64,128]{3,2,1,0:T(8,128)(2,1)S(1)}, f32[2,8,64,512]{3,2,1,0:T(8,128)S(1)}, bf16[2,640,512]{2,1,0:T(8,128)(2,1)S(1)}) custom-call(bf16[8,2,64,512]{3,2,1,0:T(8,128)(2,1)S(1)} %bitcast.38, bf16[2,64,512]{2,1,0:T(8,128)(2,1)S(1)} %collective-permute-done.low_ref, bf16[2,64,512]{2,1,0:T(8,128)(2,1)S(1)} %collective-permute-done.1.high_ref, ...), custom_call_target="tpu_custom_call" | custom-call | flops 603979776 | bytes 7938048 | tf_op jit(solution)/shard_map/pallas_call | solution.py:215
  15.6 36.1 %all_to_all.25.both_ref = bf16[32,4,64,128]{3,2,1,0:T(8,128)(2,1)S(1)} all-to-all(bf16[32,4,64,128]{3,2,1,0:T(8,128)(2,1)S(1)} %get-tuple-element.23), channel_id=1, replica_groups=mesh['wide_0'=4,'wide_1'=4,'wide_2'=2,'wide_3'=2,'narrow'=4] {'wide_0','..., dimensions={0} | all-to-all | bytes 4194304 | tf_op jit(solution)/shard_map/all_to_all | solution.py:295
  51.7 3.5 %shard_map.68 = (bf16[32,2,64,128]{3,2,1,0:T(8,128)(2,1)S(1)}, f32[64,512]{1,0:T(8,128)S(1)}) custom-call(bf16[32,4,64,128]{3,2,1,0:T(8,128)(2,1)S(1)} %all_to_all.25.both_ref, bf16[128,512]{1,0:T(8,128)(2,1)S(1)} %get-tuple-element.24.wf_ref, bf16[128,512]{1,0:T(8,128)(2,1)S(1)} %get-tuple-element.25.wb_ref), custom_call_target="tpu_custom_call" | custom-call | flops 1409286144 | bytes 3538944 | tf_op jit(solution)/shard_map/pallas_call | solution.py:215
  55.3 20.1 %all_to_all.26.back_ref = bf16[32,2,64,128]{3,2,1,0:T(8,128)(2,1)S(1)} all-to-all(bf16[32,2,64,128]{3,2,1,0:T(8,128)(2,1)S(1)} %get-tuple-element.26), channel_id=1, replica_groups=mesh['wide_0'=4,'wide_1'=4,'wide_2'=2,'wide_3'=2,'narrow'=4] {'wide_0','..., dimensions={0} | all-to-all | bytes 2097152 | tf_op jit(solution)/shard_map/all_to_all | solution.py:307
  75.4 1.3 %shard_map.69 = (bf16[8,2,64,512]{3,2,1,0:T(8,128)(2,1)S(1)}, f32[8,64,128]{2,1,0:T(8,128)S(1)}) custom-call(bf16[32,2,64,128]{3,2,1,0:T(8,128)(2,1)S(1)} %all_to_all.26.back_ref, f32[2,8,64,512]{3,2,1,0:T(8,128)S(1)} %get-tuple-element.27.slope_ref, bf16[2,640,512]{2,1,0:T(8,128)(2,1)S(1)} %get-tuple-element.28.rows_ref, ...), custom_call_target="tpu_custom_call" | custom-call | flops 603979776 | bytes 5898240 | tf_op jit(solution)/shard_map/pallas_call | solution.py:215
  76.7 13.4 %all_to_all.27.pieces_ref = f32[32,16,128]{2,1,0:T(8,128)S(1)} all-to-all(f32[32,16,128]{2,1,0:T(8,128)S(1)} %bitcast.41), channel_id=1, replica_groups=mesh['wide_0'=4,'wide_1'=4,'wide_2'=2,'wide_3'=2,'narrow'=4] {'wide_0','..., dimensions={0} | all-to-all | bytes 524288 | tf_op jit(solution)/shard_map/all_to_all | solution.py:238
  90.2 14.9 %all_to_all.28.pieces_ref = f32[8,16,128]{2,1,0:T(8,128)S(1)} all-to-all(f32[8,16,128]{2,1,0:T(8,128)S(1)} %shard_map.70), channel_id=1, replica_groups=mesh['wide_0'=4,'wide_1'=4,'wide_2'=2,'wide_3'=2,'narrow'=4] {'wide_2','..., dimensions={0} | all-to-all | bytes 131072 | tf_op jit(solution)/shard_map/all_to_all | solution.py:317
  105.0 0.7 shard_map.72
  105.8 5.0 %all-to-all-start.4 = ((f32[32,16,128]{2,1,0:T(8,128)}), f32[32,16,128]{2,1,0:T(8,128)S(1)}, u32[]{:S(2)}, u32[]{:S(2)}) async-start(f32[32,16,128]{2,1,0:T(8,128)} %shard_map.72), calls=%async_computation.4 | async-start | bytes 524288 | tf_op jit(solution)/shard_map/all_to_all | solution.py:326
  110.8 1.3 %collective-permute-start.3 = (bf16[2,64,512]{2,1,0:T(8,128)(2,1)S(1)}, bf16[2,64,512]{2,1,0:T(8,128)(2,1)S(1)}, u32[]{:S(2)}, u32[]{:S(2)}) collective-permute-start(bf16[2,64,512]{2,1,0:T(8,128)(2,1)S(1)} %get-tuple-element.43), channel_id=1, source_target_pairs={{1,0},{2,1},{3,2},{5,4},{6,5},{7,6},{9,8},{10,9},{11,10},{13,12},{... | collective-permute-start | bytes 393224 | tf_op jit(solution)/shard_map/ppermute | solution.py:29
  112.1 5.5 %collective-permute-start.2 = (bf16[2,64,512]{2,1,0:T(8,128)(2,1)S(1)}, bf16[2,64,512]{2,1,0:T(8,128)(2,1)S(1)}, u32[]{:S(2)}, u32[]{:S(2)}) collective-permute-start(bf16[2,64,512]{2,1,0:T(8,128)(2,1)S(1)} %get-tuple-element.44), channel_id=1, source_target_pairs={{0,1},{1,2},{2,3},{4,5},{5,6},{6,7},{8,9},{9,10},{10,11},{12,13},{... | collective-permute-start | bytes 393224 | tf_op jit(solution)/shard_map/ppermute | solution.py:29
  117.6 4.4 %collective-permute-done.3.high_ref = bf16[2,64,512]{2,1,0:T(8,128)(2,1)S(1)} collective-permute-done((bf16[2,64,512]{2,1,0:T(8,128)(2,1)S(1)}, bf16[2,64,512]{2,1,0:T(8,128)(2,1)S(1)}, u32[]{:S(2)}, u32[]{:S(2)}) %collective-permute-start.3) | collective-permute-done | bytes 131104 | tf_op jit(solution)/shard_map/ppermute | solution.py:29
  121.9 1.4 %shard_map.71 = bf16[8,2,64,512]{3,2,1,0:T(8,128)(2,1)S(1)} custom-call(bf16[8,2,64,512]{3,2,1,0:T(8,128)(2,1)S(1)} %get-tuple-element.30.pre_ref, bf16[2,64,512]{2,1,0:T(8,128)(2,1)S(1)} %collective-permute-done.2.low_ref, bf16[2,64,512]{2,1,0:T(8,128)(2,1)S(1)} %collective-permute-done.3.high_ref, bf16[32,2,64,128]{3,2,1,0:T(8,128)(2,1)S(1)} %bitcast.36, ...), custom_call_target="tpu_custom_call" | custom-call | flops 603979776 | bytes 3481600 | tf_op jit(solution)/shard_map/pallas_call | solution.py:215
  123.4 1.5 %copy.24 = bf16[64,2,8,512]{3,2,1,0:T(8,128)(2,1)} copy(bf16[64,2,8,512]{3,0,1,2:T(8,128)(2,1)S(1)} %bitcast.39) | data formatting | bytes 2097152
  124.9 0.9 shard_map.73
  (13 shorter events, 0.2 us)
Async XLA Ops:
  0.6 9.0 %copy-start.1 = (bf16[7,64,64]{2,1,0:T(8,128)(2,1)S(1)}, bf16[7,64,64]{2,1,0:T(8,128)(2,1)}, u32[]{:S(2)}) copy-start(bf16[7,64,64]{2,1,0:T(8,128)(2,1)} %param.7) | copy-start | bytes 172036
  0.6 9.1 %copy-start = (bf16[9,64,64]{2,1,0:T(8,128)(2,1)S(1)}, bf16[9,64,64]{2,1,0:T(8,128)(2,1)}, u32[]{:S(2)}) copy-start(bf16[9,64,64]{2,1,0:T(8,128)(2,1)} %param.6) | copy-start | bytes 221188
  2.5 11.5 %collective-permute-start.1 = (bf16[2,64,512]{2,1,0:T(8,128)(2,1)S(1)}, bf16[2,64,512]{2,1,0:T(8,128)(2,1)S(1)}, u32[]{:S(2)}, u32[]{:S(2)}) collective-permute-start(bf16[2,64,512]{2,1,0:T(8,128)(2,1)S(1)} %get-tuple-element.45), channel_id=1, source_target_pairs={{1,0},{2,1},{3,2},{5,4},{6,5},{7,6},{9,8},{10,9},{11,10},{13,12},{... | collective-permute-start | bytes 393224 | tf_op jit(solution)/shard_map/ppermute | solution.py:29
  3.8 10.2 %collective-permute-start = (bf16[2,64,512]{2,1,0:T(8,128)(2,1)S(1)}, bf16[2,64,512]{2,1,0:T(8,128)(2,1)S(1)}, u32[]{:S(2)}, u32[]{:S(2)}) collective-permute-start(bf16[2,64,512]{2,1,0:T(8,128)(2,1)S(1)} %get-tuple-element.46), channel_id=1, source_target_pairs={{0,1},{1,2},{2,3},{4,5},{5,6},{6,7},{8,9},{9,10},{10,11},{12,13},{... | collective-permute-start | bytes 393224 | tf_op jit(solution)/shard_map/ppermute | solution.py:29
  105.8 19.2 %all-to-all-start.4 = ((f32[32,16,128]{2,1,0:T(8,128)}), f32[32,16,128]{2,1,0:T(8,128)S(1)}, u32[]{:S(2)}, u32[]{:S(2)}) async-start(f32[32,16,128]{2,1,0:T(8,128)} %shard_map.72), calls=%async_computation.4 | async-start | bytes 524288 | tf_op jit(solution)/shard_map/all_to_all | solution.py:326
  110.8 11.1 %collective-permute-start.3 = (bf16[2,64,512]{2,1,0:T(8,128)(2,1)S(1)}, bf16[2,64,512]{2,1,0:T(8,128)(2,1)S(1)}, u32[]{:S(2)}, u32[]{:S(2)}) collective-permute-start(bf16[2,64,512]{2,1,0:T(8,128)(2,1)S(1)} %get-tuple-element.43), channel_id=1, source_target_pairs={{1,0},{2,1},{3,2},{5,4},{6,5},{7,6},{9,8},{10,9},{11,10},{13,12},{... | collective-permute-start | bytes 393224 | tf_op jit(solution)/shard_map/ppermute | solution.py:29
  112.1 9.8 %collective-permute-start.2 = (bf16[2,64,512]{2,1,0:T(8,128)(2,1)S(1)}, bf16[2,64,512]{2,1,0:T(8,128)(2,1)S(1)}, u32[]{:S(2)}, u32[]{:S(2)}) collective-permute-start(bf16[2,64,512]{2,1,0:T(8,128)(2,1)S(1)} %get-tuple-element.44), channel_id=1, source_target_pairs={{0,1},{1,2},{2,3},{4,5},{5,6},{6,7},{8,9},{9,10},{10,11},{12,13},{... | collective-permute-start | bytes 393224 | tf_op jit(solution)/shard_map/ppermute | solution.py:29

commit v2 on v1

--- a/solution.py
+++ b/solution.py
@@ -22,11 +22,12 @@
     return math.prod(lax.axis_size(a) for a in axes)
 
 
-def halo_rows(first, last, axis):
-    count = lax.axis_size(axis)
-    forward = [(i, i + 1) for i in range(count - 1)]
-    backward = [(i + 1, i) for i in range(count - 1)]
-    return lax.ppermute(last, axis, forward), lax.ppermute(first, axis, backward)
+def from_below(last, axis):
+    return lax.ppermute(last, axis, [(i, i + 1) for i in range(lax.axis_size(axis) - 1)])
+
+
+def from_above(first, axis):
+    return lax.ppermute(first, axis, [(i + 1, i) for i in range(lax.axis_size(axis) - 1)])
 
 
 def sigmoid(v):
@@ -225,6 +226,30 @@
     return run
 
 
+def weights_kernel(plane_ref, depth_ref, pf_ref, pb_ref, df_ref, db_ref):
+    _, width, _ = plane_ref.shape
+    none = jnp.zeros((width, width), jnp.bfloat16)
+
+    def block(row, col):
+        return (
+            slice(row * width, (row + 1) * width),
+            slice(col * width, (col + 1) * width),
+        )
+
+    def turned(tap):
+        return tap.astype(jnp.float32).T.astype(jnp.bfloat16)
+
+    for i in range(3):
+        for j in range(3):
+            pf_ref[block(j, i)] = plane_ref[3 * i + j]
+            pb_ref[block(j, 2 - i)] = turned(plane_ref[3 * i + j])
+    for a in range(2):
+        for b in range(8):
+            inside = 0 <= b - a < 7
+            df_ref[block(a, b)] = depth_ref[b - a] if inside else none
+            db_ref[block(a, b)] = turned(depth_ref[6 - (b - a)]) if inside else none
+
+
 def copies_kernel(pieces_ref, copies_ref):
     part = pieces_ref[0]
     for i in range(1, pieces_ref.shape[0]):
@@ -256,31 +281,26 @@
 
     slab = volume.transpose(2, 1, 0, 3)
     first, last = slab[0], slab[rows - 1]
-    low, high = halo_rows(first, last, "narrow")
+    low, high = from_below(last, "narrow"), from_above(first, "narrow")
 
 
     grad_blocks = out_grad.reshape(width, slabs, rows, tiles, LANES)
     grad_blocks = grad_blocks.transpose(2, 3, 1, 0, 4).reshape(blocks)
 
-    taps = plane_kernel.reshape(3, 3, width, width)
-    plane_forward = taps.transpose(1, 2, 0, 3).reshape(3 * width, 3 * width)
-    plane_backward = taps[::-1].transpose(1, 3, 0, 2).reshape(3 * width, 3 * width)
-    none = jnp.zeros((1, width, width), bf16)
-
-    def banded(tap_list):
-        upper = jnp.concatenate([tap_list, none]).transpose(1, 0, 2).reshape(width, -1)
-        lower = jnp.concatenate([none, tap_list]).transpose(1, 0, 2).reshape(width, -1)
-        return jnp.concatenate([upper, lower])
-
-    depth_forward = banded(z_axis_kernel)
-    depth_backward = banded(z_axis_kernel[::-1].transpose(0, 2, 1))
+    plane_forward, plane_backward, depth_forward, depth_backward = call(
+        weights_kernel,
+        (
+            shape((3 * width, 3 * width), bf16),
+            shape((3 * width, 3 * width), bf16),
+            shape((2 * width, 8 * width), bf16),
+            shape((2 * width, 8 * width), bf16),
+        ),
+    )(plane_kernel, z_axis_kernel)
 
     plane_flops = 2 * 9 * width * width * slabs * rows * cols
     depth_flops = plane_flops * 7 // 9
-    low, high, plane_forward, plane_backward, depth_forward, depth_backward = (
-        lax.optimization_barrier(
-            (low, high, plane_forward, plane_backward, depth_forward, depth_backward)
-        )
+    low, high, plane_forward, depth_forward, depth_backward = lax.optimization_barrier(
+        (low, high, plane_forward, depth_forward, depth_backward)
     )
     both, slope, rimmed = call(
         plane_forward_kernel,
@@ -312,7 +332,8 @@
         (pltpu.VMEM((3 * width, 3 * width), f32),),
         flops=plane_flops,
     )(back, slope, rimmed, depth_term)
-    low, high = halo_rows(pre_grad[0], pre_grad[rows - 1], "narrow")
+    low = from_below(pre_grad[rows - 1], "narrow")
+    high = from_above(pre_grad[0], "narrow")
     pieces = spread_pieces(packed)
     pieces = lax.all_to_all(copies_of(pieces, group_size(TALL)), TALL, 0, 0, tiled=True)
     pieces, plane_backward = lax.optimization_barrier((pieces, plane_backward))

time: 127 us -> 127 us (level)
  local copies, waits for them, and re-layouts: 7.54 us -> 4.18 us
  waiting for transfers between devices: 4.51 us -> 7.64 us
    ppermute x4, waiting for transfers between devices: 4.51 us -> 7.64 us  [the longest x2 7.63 us: from_above(): lax.ppermute(first, axis, [(i + 1, i) for i in range(lax.axis_size(axis)...]
    pallas_call x7 -> x8, Pallas kernels: 9.48 us -> 9.85 us  [run(): pl.pallas_call(kernel, out_shape=outs, in_specs=[vmem] * len(args), out_s...]
    unnamed x6 -> x8, local copies, waits for them, and re-layouts: 3.4 us -> 3.46 us
  transfers between devices with their start and end apart: 5 -> 5, of which waited for: 2 -> 2; matrix products, arithmetic and copies ran while one was open for 5% -> 2% of each run, Pallas kernels for 1% -> 1%
where the time goes in v2:
time: 127 us; the launch traced here: 126 us
  blocking collectives  84.5 us (67%)
  starting transfers between devices  18.9 us (15%)
  Pallas kernels  9.85 us (8%)
  waiting for transfers between devices  7.64 us (6%)
  local copies, waits for them, and re-layouts  4.18 us (3%)
    all_to_all x1, blocking collectives, on_device(): both = lax.all_to_all(both, SPREAD, 0, 0, tiled=True)  36.1 us
    all_to_all x1, blocking collectives, on_device(): back = lax.all_to_all(back_pencil, SPREAD, 0, 0, tiled=True)  20.1 us
    all_to_all x1, blocking collectives, on_device(): lax.all_to_all(copies_of(pieces, group_size(TALL)), TALL, 0, 0, tiled=True)  14.9 us
    all_to_all x1, blocking collectives, spread_pieces(): return lax.all_to_all(pieces, FLAT, 0, 0, tiled=True)  13.4 us
    ppermute x2, starting transfers between devices, from_below(): lax.ppermute(last, axis, [(i, i + 1) for i in range(lax.axis_size(axis) -...  11.3 us
    pallas_call x8, Pallas kernels, run(): pl.pallas_call(kernel, out_shape=outs, in_specs=[vmem] * len(args), out_s...  9.85 us
    ppermute x2, waiting for transfers between devices, from_above(): lax.ppermute(first, axis, [(i + 1, i) for i in range(lax.axis_size(axis)...  7.63 us
    all_to_all x1, starting transfers between devices, on_device(): lax.all_to_all(copies_of(pieces, group_size(FLAT)), FLAT, 0, 0, tiled=True)  5.02 us
  transfers between devices with their start and end apart: 5, of which 2 were waited for; matrix products, arithmetic and copies ran while one was open for 2% of the time, Pallas kernels for 1%

profile of v2, /device:TPU:2, one launch (start us, length us, event | category | flops | bytes accessed | tf_op | source)
XLA Modules:
  0.0 125.8 jit_solution(199274536193339457)
XLA Ops:
  0.6 0.0 copy-start.2
  0.6 0.0 copy-start.1
  0.7 0.0 copy-start
  0.7 1.9 %copy.11 = bf16[64,2,8,512]{3,0,1,2:T(8,128)(2,1)S(1)} copy(bf16[64,2,8,512]{3,2,1,0:T(8,128)(2,1)} %param.4) | data formatting | bytes 2097152 | tf_op args[0]
  2.6 1.3 %collective-permute-start.1 = (bf16[2,64,512]{2,1,0:T(8,128)(2,1)S(1)}, bf16[2,64,512]{2,1,0:T(8,128)(2,1)S(1)}, u32[]{:S(2)}, u32[]{:S(2)}) collective-permute-start(bf16[2,64,512]{2,1,0:T(8,128)(2,1)S(1)} %get-tuple-element.48), channel_id=1, source_target_pairs={{1,0},{2,1},{3,2},{5,4},{6,5},{7,6},{9,8},{10,9},{11,10},{13,12},{... | collective-permute-start | bytes 393224 | tf_op jit(solution)/shard_map/ppermute | solution.py:30
  3.9 5.8 %collective-permute-start = (bf16[2,64,512]{2,1,0:T(8,128)(2,1)S(1)}, bf16[2,64,512]{2,1,0:T(8,128)(2,1)S(1)}, u32[]{:S(2)}, u32[]{:S(2)}) collective-permute-start(bf16[2,64,512]{2,1,0:T(8,128)(2,1)S(1)} %get-tuple-element.49), channel_id=1, source_target_pairs={{0,1},{1,2},{2,3},{4,5},{5,6},{6,7},{8,9},{9,10},{10,11},{12,13},{... | collective-permute-start | bytes 393224 | tf_op jit(solution)/shard_map/ppermute | solution.py:26
  9.7 0.0 copy-done.2
  9.7 0.7 copy.8
  10.4 0.0 copy-done.1
  10.4 0.0 copy-done
  10.4 0.4 shard_map.67
  10.8 3.3 %collective-permute-done.1.high_ref = bf16[2,64,512]{2,1,0:T(8,128)(2,1)S(1)} collective-permute-done((bf16[2,64,512]{2,1,0:T(8,128)(2,1)S(1)}, bf16[2,64,512]{2,1,0:T(8,128)(2,1)S(1)}, u32[]{:S(2)}, u32[]{:S(2)}) %collective-permute-start.1) | collective-permute-done | bytes 131104 | tf_op jit(solution)/shard_map/ppermute | solution.py:30
  14.1 0.0 collective-permute-done.low_ref
  14.1 1.6 %shard_map.68 = (bf16[32,4,64,128]{3,2,1,0:T(8,128)(2,1)S(1)}, f32[2,8,64,512]{3,2,1,0:T(8,128)S(1)}, bf16[2,640,512]{2,1,0:T(8,128)(2,1)S(1)}) custom-call(bf16[8,2,64,512]{3,2,1,0:T(8,128)(2,1)S(1)} %bitcast.21, bf16[2,64,512]{2,1,0:T(8,128)(2,1)S(1)} %collective-permute-done.low_ref, bf16[2,64,512]{2,1,0:T(8,128)(2,1)S(1)} %collective-permute-done.1.high_ref, ...), custom_call_target="tpu_custom_call" | custom-call | flops 603979776 | bytes 7938048 | tf_op jit(solution)/shard_map/pallas_call | solution.py:216
  15.7 36.1 %all_to_all.25.both_ref = bf16[32,4,64,128]{3,2,1,0:T(8,128)(2,1)S(1)} all-to-all(bf16[32,4,64,128]{3,2,1,0:T(8,128)(2,1)S(1)} %get-tuple-element.29), channel_id=1, replica_groups=mesh['wide_0'=4,'wide_1'=4,'wide_2'=2,'wide_3'=2,'narrow'=4] {'wide_0','..., dimensions={0} | all-to-all | bytes 4194304 | tf_op jit(solution)/shard_map/all_to_all | solution.py:315
  51.8 3.5 %shard_map.69 = (bf16[32,2,64,128]{3,2,1,0:T(8,128)(2,1)S(1)}, f32[64,512]{1,0:T(8,128)S(1)}) custom-call(bf16[32,4,64,128]{3,2,1,0:T(8,128)(2,1)S(1)} %all_to_all.25.both_ref, bf16[128,512]{1,0:T(8,128)(2,1)S(1)} %get-tuple-element.30.wf_ref, bf16[128,512]{1,0:T(8,128)(2,1)S(1)} %get-tuple-element.31.wb_ref), custom_call_target="tpu_custom_call" | custom-call | flops 1409286144 | bytes 3538944 | tf_op jit(solution)/shard_map/pallas_call | solution.py:216
  55.3 20.1 %all_to_all.26.back_ref = bf16[32,2,64,128]{3,2,1,0:T(8,128)(2,1)S(1)} all-to-all(bf16[32,2,64,128]{3,2,1,0:T(8,128)(2,1)S(1)} %get-tuple-element.32), channel_id=1, replica_groups=mesh['wide_0'=4,'wide_1'=4,'wide_2'=2,'wide_3'=2,'narrow'=4] {'wide_0','..., dimensions={0} | all-to-all | bytes 2097152 | tf_op jit(solution)/shard_map/all_to_all | solution.py:327
  75.4 1.3 %shard_map.70 = (bf16[8,2,64,512]{3,2,1,0:T(8,128)(2,1)S(1)}, f32[8,64,128]{2,1,0:T(8,128)S(1)}) custom-call(bf16[32,2,64,128]{3,2,1,0:T(8,128)(2,1)S(1)} %all_to_all.26.back_ref, f32[2,8,64,512]{3,2,1,0:T(8,128)S(1)} %get-tuple-element.33.slope_ref, bf16[2,640,512]{2,1,0:T(8,128)(2,1)S(1)} %get-tuple-element.34.rows_ref, ...), custom_call_target="tpu_custom_call" | custom-call | flops 603979776 | bytes 5898240 | tf_op jit(solution)/shard_map/pallas_call | solution.py:216
  76.7 13.4 %all_to_all.27.pieces_ref = f32[32,16,128]{2,1,0:T(8,128)S(1)} all-to-all(f32[32,16,128]{2,1,0:T(8,128)S(1)} %bitcast.24), channel_id=1, replica_groups=mesh['wide_0'=4,'wide_1'=4,'wide_2'=2,'wide_3'=2,'narrow'=4] {'wide_0','..., dimensions={0} | all-to-all | bytes 524288 | tf_op jit(solution)/shard_map/all_to_all | solution.py:263
  90.2 14.9 %all_to_all.28.pieces_ref = f32[8,16,128]{2,1,0:T(8,128)S(1)} all-to-all(f32[8,16,128]{2,1,0:T(8,128)S(1)} %shard_map.71), channel_id=1, replica_groups=mesh['wide_0'=4,'wide_1'=4,'wide_2'=2,'wide_3'=2,'narrow'=4] {'wide_2','..., dimensions={0} | all-to-all | bytes 131072 | tf_op jit(solution)/shard_map/all_to_all | solution.py:338
  105.1 0.7 shard_map.73
  105.8 5.0 %all-to-all-start.4 = ((f32[32,16,128]{2,1,0:T(8,128)}), f32[32,16,128]{2,1,0:T(8,128)S(1)}, u32[]{:S(2)}, u32[]{:S(2)}) async-start(f32[32,16,128]{2,1,0:T(8,128)} %shard_map.73), calls=%async_computation.4 | async-start | bytes 524288 | tf_op jit(solution)/shard_map/all_to_all | solution.py:347
  110.9 1.3 %collective-permute-start.3 = (bf16[2,64,512]{2,1,0:T(8,128)(2,1)S(1)}, bf16[2,64,512]{2,1,0:T(8,128)(2,1)S(1)}, u32[]{:S(2)}, u32[]{:S(2)}) collective-permute-start(bf16[2,64,512]{2,1,0:T(8,128)(2,1)S(1)} %get-tuple-element.46), channel_id=1, source_target_pairs={{1,0},{2,1},{3,2},{5,4},{6,5},{7,6},{9,8},{10,9},{11,10},{13,12},{... | collective-permute-start | bytes 393224 | tf_op jit(solution)/shard_map/ppermute | solution.py:30
  112.2 5.5 %collective-permute-start.2 = (bf16[2,64,512]{2,1,0:T(8,128)(2,1)S(1)}, bf16[2,64,512]{2,1,0:T(8,128)(2,1)S(1)}, u32[]{:S(2)}, u32[]{:S(2)}) collective-permute-start(bf16[2,64,512]{2,1,0:T(8,128)(2,1)S(1)} %get-tuple-element.47), channel_id=1, source_target_pairs={{0,1},{1,2},{2,3},{4,5},{5,6},{6,7},{8,9},{9,10},{10,11},{12,13},{... | collective-permute-start | bytes 393224 | tf_op jit(solution)/shard_map/ppermute | solution.py:26
  117.6 4.4 %collective-permute-done.3.high_ref = bf16[2,64,512]{2,1,0:T(8,128)(2,1)S(1)} collective-permute-done((bf16[2,64,512]{2,1,0:T(8,128)(2,1)S(1)}, bf16[2,64,512]{2,1,0:T(8,128)(2,1)S(1)}, u32[]{:S(2)}, u32[]{:S(2)}) %collective-permute-start.3) | collective-permute-done | bytes 131104 | tf_op jit(solution)/shard_map/ppermute | solution.py:30
  122.0 0.0 collective-permute-done.2.low_ref
  122.0 1.4 %shard_map.72 = bf16[8,2,64,512]{3,2,1,0:T(8,128)(2,1)S(1)} custom-call(bf16[8,2,64,512]{3,2,1,0:T(8,128)(2,1)S(1)} %get-tuple-element.36.pre_ref, bf16[2,64,512]{2,1,0:T(8,128)(2,1)S(1)} %collective-permute-done.2.low_ref, bf16[2,64,512]{2,1,0:T(8,128)(2,1)S(1)} %collective-permute-done.3.high_ref, bf16[32,2,64,128]{3,2,1,0:T(8,128)(2,1)S(1)} %bitcast.19, ...), custom_call_target="tpu_custom_call" | custom-call | flops 603979776 | bytes 3481600 | tf_op jit(solution)/shard_map/pallas_call | solution.py:216
  123.4 1.5 %copy.9 = bf16[64,2,8,512]{3,2,1,0:T(8,128)(2,1)} copy(bf16[64,2,8,512]{3,0,1,2:T(8,128)(2,1)S(1)} %bitcast.22) | data formatting | bytes 2097152
  125.0 0.0 all-to-all-done.4
  125.0 0.9 shard_map.74
  (3 shorter events, 0.1 us)
Async XLA Ops:
  0.6 9.1 %copy-start.2 = (bf16[64,2,8,512]{3,2,1,0:T(8,128)(2,1)S(1)}, bf16[64,2,8,512]{3,2,1,0:T(8,128)(2,1)}, u32[]{:S(2)}) copy-start(bf16[64,2,8,512]{3,2,1,0:T(8,128)(2,1)} %param.5) | copy-start | bytes 3145732
  0.6 9.8 %copy-start.1 = (bf16[7,64,64]{2,1,0:T(8,128)(2,1)S(1)}, bf16[7,64,64]{2,1,0:T(8,128)(2,1)}, u32[]{:S(2)}) copy-start(bf16[7,64,64]{2,1,0:T(8,128)(2,1)} %depth_ref.1) | copy-start | bytes 172036
  0.7 9.8 %copy-start = (bf16[9,64,64]{2,1,0:T(8,128)(2,1)S(1)}, bf16[9,64,64]{2,1,0:T(8,128)(2,1)}, u32[]{:S(2)}) copy-start(bf16[9,64,64]{2,1,0:T(8,128)(2,1)} %plane_ref.1) | copy-start | bytes 221188
  2.6 11.5 %collective-permute-start.1 = (bf16[2,64,512]{2,1,0:T(8,128)(2,1)S(1)}, bf16[2,64,512]{2,1,0:T(8,128)(2,1)S(1)}, u32[]{:S(2)}, u32[]{:S(2)}) collective-permute-start(bf16[2,64,512]{2,1,0:T(8,128)(2,1)S(1)} %get-tuple-element.48), channel_id=1, source_target_pairs={{1,0},{2,1},{3,2},{5,4},{6,5},{7,6},{9,8},{10,9},{11,10},{13,12},{... | collective-permute-start | bytes 393224 | tf_op jit(solution)/shard_map/ppermute | solution.py:30
  3.9 10.2 %collective-permute-start = (bf16[2,64,512]{2,1,0:T(8,128)(2,1)S(1)}, bf16[2,64,512]{2,1,0:T(8,128)(2,1)S(1)}, u32[]{:S(2)}, u32[]{:S(2)}) collective-permute-start(bf16[2,64,512]{2,1,0:T(8,128)(2,1)S(1)} %get-tuple-element.49), channel_id=1, source_target_pairs={{0,1},{1,2},{2,3},{4,5},{5,6},{6,7},{8,9},{9,10},{10,11},{12,13},{... | collective-permute-start | bytes 393224 | tf_op jit(solution)/shard_map/ppermute | solution.py:26
  105.8 19.2 %all-to-all-start.4 = ((f32[32,16,128]{2,1,0:T(8,128)}), f32[32,16,128]{2,1,0:T(8,128)S(1)}, u32[]{:S(2)}, u32[]{:S(2)}) async-start(f32[32,16,128]{2,1,0:T(8,128)} %shard_map.73), calls=%async_computation.4 | async-start | bytes 524288 | tf_op jit(solution)/shard_map/all_to_all | solution.py:347
  110.9 11.1 %collective-permute-start.3 = (bf16[2,64,512]{2,1,0:T(8,128)(2,1)S(1)}, bf16[2,64,512]{2,1,0:T(8,128)(2,1)S(1)}, u32[]{:S(2)}, u32[]{:S(2)}) collective-permute-start(bf16[2,64,512]{2,1,0:T(8,128)(2,1)S(1)} %get-tuple-element.46), channel_id=1, source_target_pairs={{1,0},{2,1},{3,2},{5,4},{6,5},{7,6},{9,8},{10,9},{11,10},{13,12},{... | collective-permute-start | bytes 393224 | tf_op jit(solution)/shard_map/ppermute | solution.py:30
  112.2 9.8 %collective-permute-start.2 = (bf16[2,64,512]{2,1,0:T(8,128)(2,1)S(1)}, bf16[2,64,512]{2,1,0:T(8,128)(2,1)S(1)}, u32[]{:S(2)}, u32[]{:S(2)}) collective-permute-start(bf16[2,64,512]{2,1,0:T(8,128)(2,1)S(1)} %get-tuple-element.47), channel_id=1, source_target_pairs={{0,1},{1,2},{2,3},{4,5},{5,6},{6,7},{8,9},{9,10},{10,11},{12,13},{... | collective-permute-start | bytes 393224 | tf_op jit(solution)/shard_map/ppermute | solution.py:26

commit v3 on v2

--- a/solution.py
+++ b/solution.py
@@ -11,9 +11,9 @@
 
 LANES = 128
 UNROLL = 16
-SPREAD = ("wide_0", "wide_2", "wide_1")
+SPREAD = ("wide_2", "wide_0", "wide_1")
 WIDE = ("wide_0", "wide_1", "wide_2", "wide_3")
-FLAT = ("wide_0", "wide_1", "wide_3")
+FLAT = ("wide_3", "wide_0", "wide_1")
 TALL = ("wide_2", "narrow")
 FACTORS = (4, 4, 2, 2)
 
@@ -82,8 +82,7 @@
 
 
 def peer_of(position, inner, outer):
-    z, rest = position % inner, position // inner
-    return (rest // outer) * (inner * outer) + z * outer + rest % outer
+    return (position % inner) * outer + position // inner
 
 
 def depth_kernel(inner, outer, both_ref, wf_ref, wb_ref, out_ref, dw_ref, a_ref, d_ref, acc_ref):
@@ -315,7 +314,7 @@
     both = lax.all_to_all(both, SPREAD, 0, 0, tiled=True)
     span = (peers + 6) * width
     back_pencil, depth_term = call(
-        functools.partial(depth_kernel, lax.axis_size("wide_2"), lax.axis_size("wide_1")),
+        functools.partial(depth_kernel, lax.axis_size("wide_2"), group_size(SPREAD[1:])),
         (shape(blocks, bf16), shape((width, 8 * width), f32)),
         (
             pltpu.VMEM((span, slabs * LANES), bf16),

time: 127 us -> 127 us (level)
  no operation moved by 1% of the time
where the time goes in v3:
time: 127 us; the launch traced here: 126 us
  blocking collectives  84.8 us (67%)
  starting transfers between devices  18.7 us (15%)
  Pallas kernels  9.68 us (8%)
  waiting for transfers between devices  7.74 us (6%)
  local copies, waits for them, and re-layouts  4.18 us (3%)
    all_to_all x1, blocking collectives, on_device(): both = lax.all_to_all(both, SPREAD, 0, 0, tiled=True)  36.6 us
    all_to_all x1, blocking collectives, on_device(): back = lax.all_to_all(back_pencil, SPREAD, 0, 0, tiled=True)  20.4 us
    all_to_all x1, blocking collectives, on_device(): lax.all_to_all(copies_of(pieces, group_size(TALL)), TALL, 0, 0, tiled=True)  14.6 us
    all_to_all x1, blocking collectives, spread_pieces(): return lax.all_to_all(pieces, FLAT, 0, 0, tiled=True)  13.1 us
    ppermute x2, starting transfers between devices, from_below(): lax.ppermute(last, axis, [(i, i + 1) for i in range(lax.axis_size(axis) -...  11.3 us
    pallas_call x8, Pallas kernels, run(): pl.pallas_call(kernel, out_shape=outs, in_specs=[vmem] * len(args), out_s...  9.68 us
    ppermute x2, waiting for transfers between devices, from_above(): lax.ppermute(first, axis, [(i + 1, i) for i in range(lax.axis_size(axis)...  7.73 us
    all_to_all x1, starting transfers between devices, on_device(): lax.all_to_all(copies_of(pieces, group_size(FLAT)), FLAT, 0, 0, tiled=True)  4.89 us
  transfers between devices with their start and end apart: 5, of which 2 were waited for; matrix products, arithmetic and copies ran while one was open for 2% of the time, Pallas kernels for 1%

profile of v3, /device:TPU:2, one launch (start us, length us, event | category | flops | bytes accessed | tf_op | source)
XLA Modules:
  0.0 125.9 jit_solution(16853314442701706876)
XLA Ops:
  0.6 0.0 copy-start.2
  0.6 0.0 copy-start.1
  0.7 0.0 copy-start
  0.7 1.9 %copy.11 = bf16[64,2,8,512]{3,0,1,2:T(8,128)(2,1)S(1)} copy(bf16[64,2,8,512]{3,2,1,0:T(8,128)(2,1)} %param.4) | data formatting | bytes 2097152 | tf_op args[0]
  2.6 1.3 %collective-permute-start.1 = (bf16[2,64,512]{2,1,0:T(8,128)(2,1)S(1)}, bf16[2,64,512]{2,1,0:T(8,128)(2,1)S(1)}, u32[]{:S(2)}, u32[]{:S(2)}) collective-permute-start(bf16[2,64,512]{2,1,0:T(8,128)(2,1)S(1)} %get-tuple-element.48), channel_id=1, source_target_pairs={{1,0},{2,1},{3,2},{5,4},{6,5},{7,6},{9,8},{10,9},{11,10},{13,12},{... | collective-permute-start | bytes 393224 | tf_op jit(solution)/shard_map/ppermute | solution.py:30
  3.9 5.8 %collective-permute-start = (bf16[2,64,512]{2,1,0:T(8,128)(2,1)S(1)}, bf16[2,64,512]{2,1,0:T(8,128)(2,1)S(1)}, u32[]{:S(2)}, u32[]{:S(2)}) collective-permute-start(bf16[2,64,512]{2,1,0:T(8,128)(2,1)S(1)} %get-tuple-element.49), channel_id=1, source_target_pairs={{0,1},{1,2},{2,3},{4,5},{5,6},{6,7},{8,9},{9,10},{10,11},{12,13},{... | collective-permute-start | bytes 393224 | tf_op jit(solution)/shard_map/ppermute | solution.py:26
  9.7 0.0 copy-done.2
  9.7 0.7 copy.8
  10.4 0.0 copy-done.1
  10.4 0.0 copy-done
  10.4 0.4 shard_map.67
  10.8 3.3 %collective-permute-done.1.high_ref = bf16[2,64,512]{2,1,0:T(8,128)(2,1)S(1)} collective-permute-done((bf16[2,64,512]{2,1,0:T(8,128)(2,1)S(1)}, bf16[2,64,512]{2,1,0:T(8,128)(2,1)S(1)}, u32[]{:S(2)}, u32[]{:S(2)}) %collective-permute-start.1) | collective-permute-done | bytes 131104 | tf_op jit(solution)/shard_map/ppermute | solution.py:30
  14.1 0.0 collective-permute-done.low_ref
  14.1 1.6 %shard_map.68 = (bf16[32,4,64,128]{3,2,1,0:T(8,128)(2,1)S(1)}, f32[2,8,64,512]{3,2,1,0:T(8,128)S(1)}, bf16[2,640,512]{2,1,0:T(8,128)(2,1)S(1)}) custom-call(bf16[8,2,64,512]{3,2,1,0:T(8,128)(2,1)S(1)} %bitcast.21, bf16[2,64,512]{2,1,0:T(8,128)(2,1)S(1)} %collective-permute-done.low_ref, bf16[2,64,512]{2,1,0:T(8,128)(2,1)S(1)} %collective-permute-done.1.high_ref, ...), custom_call_target="tpu_custom_call" | custom-call | flops 603979776 | bytes 7938048 | tf_op jit(solution)/shard_map/pallas_call | solution.py:215
  15.7 36.6 %all_to_all.25.both_ref = bf16[32,4,64,128]{3,2,1,0:T(8,128)(2,1)S(1)} all-to-all(bf16[32,4,64,128]{3,2,1,0:T(8,128)(2,1)S(1)} %get-tuple-element.29), channel_id=1, replica_groups=mesh['wide_0'=4,'wide_1'=4,'wide_2'=2,'wide_3'=2,'narrow'=4] {'wide_2','..., dimensions={0} | all-to-all | bytes 4194304 | tf_op jit(solution)/shard_map/all_to_all | solution.py:314
  52.3 3.4 %shard_map.69 = (bf16[32,2,64,128]{3,2,1,0:T(8,128)(2,1)S(1)}, f32[64,512]{1,0:T(8,128)S(1)}) custom-call(bf16[32,4,64,128]{3,2,1,0:T(8,128)(2,1)S(1)} %all_to_all.25.both_ref, bf16[128,512]{1,0:T(8,128)(2,1)S(1)} %get-tuple-element.30.wf_ref, bf16[128,512]{1,0:T(8,128)(2,1)S(1)} %get-tuple-element.31.wb_ref), custom_call_target="tpu_custom_call" | custom-call | flops 1409286144 | bytes 3538944 | tf_op jit(solution)/shard_map/pallas_call | solution.py:215
  55.7 20.4 %all_to_all.26.back_ref = bf16[32,2,64,128]{3,2,1,0:T(8,128)(2,1)S(1)} all-to-all(bf16[32,2,64,128]{3,2,1,0:T(8,128)(2,1)S(1)} %get-tuple-element.32), channel_id=1, replica_groups=mesh['wide_0'=4,'wide_1'=4,'wide_2'=2,'wide_3'=2,'narrow'=4] {'wide_2','..., dimensions={0} | all-to-all | bytes 2097152 | tf_op jit(solution)/shard_map/all_to_all | solution.py:326
  76.1 1.3 %shard_map.70 = (bf16[8,2,64,512]{3,2,1,0:T(8,128)(2,1)S(1)}, f32[8,64,128]{2,1,0:T(8,128)S(1)}) custom-call(bf16[32,2,64,128]{3,2,1,0:T(8,128)(2,1)S(1)} %all_to_all.26.back_ref, f32[2,8,64,512]{3,2,1,0:T(8,128)S(1)} %get-tuple-element.33.slope_ref, bf16[2,640,512]{2,1,0:T(8,128)(2,1)S(1)} %get-tuple-element.34.rows_ref, ...), custom_call_target="tpu_custom_call" | custom-call | flops 603979776 | bytes 5898240 | tf_op jit(solution)/shard_map/pallas_call | solution.py:215
  77.4 13.1 %all_to_all.27.pieces_ref = f32[32,16,128]{2,1,0:T(8,128)S(1)} all-to-all(f32[32,16,128]{2,1,0:T(8,128)S(1)} %bitcast.24), channel_id=1, replica_groups=mesh['wide_0'=4,'wide_1'=4,'wide_2'=2,'wide_3'=2,'narrow'=4] {'wide_3','..., dimensions={0} | all-to-all | bytes 524288 | tf_op jit(solution)/shard_map/all_to_all | solution.py:262
  90.5 14.6 %all_to_all.28.pieces_ref = f32[8,16,128]{2,1,0:T(8,128)S(1)} all-to-all(f32[8,16,128]{2,1,0:T(8,128)S(1)} %shard_map.71), channel_id=1, replica_groups=mesh['wide_0'=4,'wide_1'=4,'wide_2'=2,'wide_3'=2,'narrow'=4] {'wide_2','..., dimensions={0} | all-to-all | bytes 131072 | tf_op jit(solution)/shard_map/all_to_all | solution.py:337
  105.2 0.7 shard_map.73
  105.9 4.9 %all-to-all-start.4 = ((f32[32,16,128]{2,1,0:T(8,128)}), f32[32,16,128]{2,1,0:T(8,128)S(1)}, u32[]{:S(2)}, u32[]{:S(2)}) async-start(f32[32,16,128]{2,1,0:T(8,128)} %shard_map.73), calls=%async_computation.4 | async-start | bytes 524288 | tf_op jit(solution)/shard_map/all_to_all | solution.py:346
  110.8 1.3 %collective-permute-start.3 = (bf16[2,64,512]{2,1,0:T(8,128)(2,1)S(1)}, bf16[2,64,512]{2,1,0:T(8,128)(2,1)S(1)}, u32[]{:S(2)}, u32[]{:S(2)}) collective-permute-start(bf16[2,64,512]{2,1,0:T(8,128)(2,1)S(1)} %get-tuple-element.46), channel_id=1, source_target_pairs={{1,0},{2,1},{3,2},{5,4},{6,5},{7,6},{9,8},{10,9},{11,10},{13,12},{... | collective-permute-start | bytes 393224 | tf_op jit(solution)/shard_map/ppermute | solution.py:30
  112.1 5.5 %collective-permute-start.2 = (bf16[2,64,512]{2,1,0:T(8,128)(2,1)S(1)}, bf16[2,64,512]{2,1,0:T(8,128)(2,1)S(1)}, u32[]{:S(2)}, u32[]{:S(2)}) collective-permute-start(bf16[2,64,512]{2,1,0:T(8,128)(2,1)S(1)} %get-tuple-element.47), channel_id=1, source_target_pairs={{0,1},{1,2},{2,3},{4,5},{5,6},{6,7},{8,9},{9,10},{10,11},{12,13},{... | collective-permute-start | bytes 393224 | tf_op jit(solution)/shard_map/ppermute | solution.py:26
  117.6 4.5 %collective-permute-done.3.high_ref = bf16[2,64,512]{2,1,0:T(8,128)(2,1)S(1)} collective-permute-done((bf16[2,64,512]{2,1,0:T(8,128)(2,1)S(1)}, bf16[2,64,512]{2,1,0:T(8,128)(2,1)S(1)}, u32[]{:S(2)}, u32[]{:S(2)}) %collective-permute-start.3) | collective-permute-done | bytes 131104 | tf_op jit(solution)/shard_map/ppermute | solution.py:30
  122.1 0.0 collective-permute-done.2.low_ref
  122.1 1.4 %shard_map.72 = bf16[8,2,64,512]{3,2,1,0:T(8,128)(2,1)S(1)} custom-call(bf16[8,2,64,512]{3,2,1,0:T(8,128)(2,1)S(1)} %get-tuple-element.36.pre_ref, bf16[2,64,512]{2,1,0:T(8,128)(2,1)S(1)} %collective-permute-done.2.low_ref, bf16[2,64,512]{2,1,0:T(8,128)(2,1)S(1)} %collective-permute-done.3.high_ref, bf16[32,2,64,128]{3,2,1,0:T(8,128)(2,1)S(1)} %bitcast.19, ...), custom_call_target="tpu_custom_call" | custom-call | flops 603979776 | bytes 3481600 | tf_op jit(solution)/shard_map/pallas_call | solution.py:215
  123.5 1.5 %copy.9 = bf16[64,2,8,512]{3,2,1,0:T(8,128)(2,1)} copy(bf16[64,2,8,512]{3,0,1,2:T(8,128)(2,1)S(1)} %bitcast.22) | data formatting | bytes 2097152
  125.0 0.0 all-to-all-done.4
  125.0 0.9 shard_map.74
  (3 shorter events, 0.1 us)
Async XLA Ops:
  0.6 9.1 %copy-start.2 = (bf16[64,2,8,512]{3,2,1,0:T(8,128)(2,1)S(1)}, bf16[64,2,8,512]{3,2,1,0:T(8,128)(2,1)}, u32[]{:S(2)}) copy-start(bf16[64,2,8,512]{3,2,1,0:T(8,128)(2,1)} %param.5) | copy-start | bytes 3145732
  0.6 9.8 %copy-start.1 = (bf16[7,64,64]{2,1,0:T(8,128)(2,1)S(1)}, bf16[7,64,64]{2,1,0:T(8,128)(2,1)}, u32[]{:S(2)}) copy-start(bf16[7,64,64]{2,1,0:T(8,128)(2,1)} %depth_ref.1) | copy-start | bytes 172036
  0.7 9.8 %copy-start = (bf16[9,64,64]{2,1,0:T(8,128)(2,1)S(1)}, bf16[9,64,64]{2,1,0:T(8,128)(2,1)}, u32[]{:S(2)}) copy-start(bf16[9,64,64]{2,1,0:T(8,128)(2,1)} %plane_ref.1) | copy-start | bytes 221188
  2.6 11.5 %collective-permute-start.1 = (bf16[2,64,512]{2,1,0:T(8,128)(2,1)S(1)}, bf16[2,64,512]{2,1,0:T(8,128)(2,1)S(1)}, u32[]{:S(2)}, u32[]{:S(2)}) collective-permute-start(bf16[2,64,512]{2,1,0:T(8,128)(2,1)S(1)} %get-tuple-element.48), channel_id=1, source_target_pairs={{1,0},{2,1},{3,2},{5,4},{6,5},{7,6},{9,8},{10,9},{11,10},{13,12},{... | collective-permute-start | bytes 393224 | tf_op jit(solution)/shard_map/ppermute | solution.py:30
  3.9 10.2 %collective-permute-start = (bf16[2,64,512]{2,1,0:T(8,128)(2,1)S(1)}, bf16[2,64,512]{2,1,0:T(8,128)(2,1)S(1)}, u32[]{:S(2)}, u32[]{:S(2)}) collective-permute-start(bf16[2,64,512]{2,1,0:T(8,128)(2,1)S(1)} %get-tuple-element.49), channel_id=1, source_target_pairs={{0,1},{1,2},{2,3},{4,5},{5,6},{6,7},{8,9},{9,10},{10,11},{12,13},{... | collective-permute-start | bytes 393224 | tf_op jit(solution)/shard_map/ppermute | solution.py:26
  105.9 19.1 %all-to-all-start.4 = ((f32[32,16,128]{2,1,0:T(8,128)}), f32[32,16,128]{2,1,0:T(8,128)S(1)}, u32[]{:S(2)}, u32[]{:S(2)}) async-start(f32[32,16,128]{2,1,0:T(8,128)} %shard_map.73), calls=%async_computation.4 | async-start | bytes 524288 | tf_op jit(solution)/shard_map/all_to_all | solution.py:346
  110.8 11.2 %collective-permute-start.3 = (bf16[2,64,512]{2,1,0:T(8,128)(2,1)S(1)}, bf16[2,64,512]{2,1,0:T(8,128)(2,1)S(1)}, u32[]{:S(2)}, u32[]{:S(2)}) collective-permute-start(bf16[2,64,512]{2,1,0:T(8,128)(2,1)S(1)} %get-tuple-element.46), channel_id=1, source_target_pairs={{1,0},{2,1},{3,2},{5,4},{6,5},{7,6},{9,8},{10,9},{11,10},{13,12},{... | collective-permute-start | bytes 393224 | tf_op jit(solution)/shard_map/ppermute | solution.py:30
  112.1 9.9 %collective-permute-start.2 = (bf16[2,64,512]{2,1,0:T(8,128)(2,1)S(1)}, bf16[2,64,512]{2,1,0:T(8,128)(2,1)S(1)}, u32[]{:S(2)}, u32[]{:S(2)}) collective-permute-start(bf16[2,64,512]{2,1,0:T(8,128)(2,1)S(1)} %get-tuple-element.47), channel_id=1, source_target_pairs={{0,1},{1,2},{2,3},{4,5},{5,6},{6,7},{8,9},{9,10},{10,11},{12,13},{... | collective-permute-start | bytes 393224 | tf_op jit(solution)/shard_map/ppermute | solution.py:26
